TPU v7x, 256 devices: a whole 4x4x8 slice. The times are simulated.
256 devices in a mesh: sub: 4 (over y), row: 4 (over x_lo, core), col: 16 (over z, x_hi).
Axes of the slice: x: 4 (x_hi: 2, x_lo: 2; x = x_hi * 2 + x_lo), y: 4, z: 8, core: 2. Of those that a mesh axis runs over, the one named last changes fastest.
Arguments:
- pressure_rhs: float32 [3, 4, 4096, 128], P(None, 'sub', 'col'), may hold values from -6 to 6
- diag_inverse: float32 [4, 4096, 7, 4096], P('sub', 'row', None, 'col'), as said below
- factor_blocks: float32 [3, 4, 2048, 4096], P(None, 'sub', 'col', 'row'), may hold values from -0.09375 to 0.09375
- row_lists: int32 [3, 4, 2048], P(None, 'sub', 'col'), may hold values from 0 to 16383, as said below
Outputs:
- solution: float32 [3, 4, 4096, 128], P(None, 'sub', 'col')
Inputs may be any that keep to these rules, and one draw needn't show every extreme that they name: `diag_inverse`: in slot 2^l - 1 + q the block of row panel s is zero where q > s mod 2^l, and lower triangular with diagonal entries between 0.5 and 2 where q = s mod 2^l. row_lists[t, s, k] = q * 4096 + 2 k + e with e 0 or 1 and q below 2^m, m the upper level of pair t; entry 0 of every list is 0 and entry 2047 is 2^m * 4096 - 1.
All inputs are finite; a program needn't handle non-finite values.
Results may differ from a plain program's by a relative error of at most 0.00012.
Values sent between devices are 32-bit elements; how exact they have to be, the bound alone decides.
No kernel may reach another device: no remote copies, remote signals or barrier semaphores. Data moves between devices by JAX's collectives and lax.ppermute only.
A program may use at most 64 MiB of HBM per device.

v0:
```python
import jax
import jax.numpy as jnp
from jax import lax
from jax.sharding import PartitionSpec as P

S = 4096
NRHS = 128
exact_mode = lax.Precision.HIGHEST


def swapped(value, axis, bit):
    mask = 2**bit
    pairs = [(source, source ^ mask) for source in range(lax.axis_size(axis))]
    return lax.ppermute(value, axis, pairs)


def pair_slot(low_level, high_level, level_count):
    return (
        low_level * (level_count - 1)
        - low_level * (low_level - 1) // 2
        + high_level
        - low_level
        - 1
    )


def local_rows(row_lists, slot_index, col_block):
    targets = row_lists[slot_index, 0]
    panel_of = targets // S
    offset_in = targets % S - lax.axis_index("col") * col_block
    return panel_of * col_block + offset_in


def pick_half(stacked, which):
    return lax.dynamic_index_in_dim(stacked, which, 0, keepdims=False)


def fold_halves(values, level_num):
    sub_place = lax.axis_index("sub")
    for bit_index in reversed(range(level_num)):
        own_bit = sub_place >> bit_index & 1
        halves = values.reshape((2, values.shape[0] // 2) + values.shape[1:])
        keeper = pick_half(halves, own_bit)
        giving = pick_half(halves, 1 - own_bit)
        values = keeper + swapped(giving, "sub", bit_index)
    return values


def spread_panels(values, level_num):
    sub_place = lax.axis_index("sub")
    for bit_index in range(level_num):
        own_bit = sub_place >> bit_index & 1
        partner = swapped(values, "sub", bit_index)
        values = jnp.where(
            own_bit == 0,
            jnp.concatenate([values, partner], 0),
            jnp.concatenate([partner, values], 0),
        )
    return values


def separator_sum(values, level_num, own_rhs):
    own_part = fold_halves(values, level_num)[0]
    own_part = lax.psum(own_part, "row")
    if own_rhs is not None:
        own_part = own_rhs - own_part
    return spread_panels(own_part[None], level_num)


def on_device(pressure_rhs, diag_inverse, factor_blocks, row_lists):
    level_count = pressure_rhs.shape[0]
    col_block = pressure_rhs.shape[2]
    row_block = diag_inverse.shape[1]
    pending = {}
    for high_level in range(1, level_count):
        pending[high_level] = jnp.zeros((2**high_level * col_block, NRHS), jnp.float32)
    solved = []
    for level_num in range(level_count):
        span_size = 2**level_num
        own_rhs = pressure_rhs[level_num, 0]
        if level_num == 0:
            gathered = own_rhs[None]
        else:
            gathered = separator_sum(
                pending[level_num].reshape(span_size, col_block, NRHS), level_num, own_rhs
            )
        diag_blocks = diag_inverse[0, :, span_size - 1 : 2 * span_size - 1, :]
        column_part = jnp.einsum("ias,asn->in", diag_blocks, gathered, precision=exact_mode)
        solved_panel = lax.psum(column_part, "col")
        solved.append(solved_panel)
        for high_level in range(level_num + 1, level_count):
            slot_index = pair_slot(level_num, high_level, level_count)
            update_rows = jnp.dot(factor_blocks[slot_index, 0], solved_panel, precision=exact_mode)
            where_to = local_rows(row_lists, slot_index, col_block)
            pending[high_level] = pending[high_level].at[where_to].add(update_rows)
    finished = [None] * level_count
    for level_num in reversed(range(level_count)):
        span_size = 2**level_num
        residue = solved[level_num]
        if level_num < level_count - 1:
            correction = jnp.zeros((row_block, NRHS), jnp.float32)
            for high_level in range(level_num + 1, level_count):
                slot_index = pair_slot(level_num, high_level, level_count)
                where_from = local_rows(row_lists, slot_index, col_block)
                picked = finished[high_level].reshape(-1, NRHS)[where_from]
                correction = correction + jnp.einsum(
                    "ks,kn->sn", factor_blocks[slot_index, 0], picked, precision=exact_mode
                )
            residue = residue - lax.psum(correction, "col")
        diag_blocks = diag_inverse[0, :, span_size - 1 : 2 * span_size - 1, :]
        pieces = jnp.einsum("ias,in->asn", diag_blocks, residue, precision=exact_mode)
        finished[level_num] = separator_sum(pieces, level_num, None)
    sub_place = lax.axis_index("sub")
    outputs = []
    for level_num in range(level_count):
        outputs.append(
            lax.dynamic_index_in_dim(
                finished[level_num], sub_place % 2**level_num, 0, keepdims=False
            )
        )
    return jnp.stack(outputs)[:, None]


def solution(mesh):
    in_specs = (
        P(None, "sub", "col", None),
        P("sub", "row", None, "col"),
        P(None, "sub", "col", "row"),
        P(None, "sub", "col"),
    )
    out_specs = P(None, "sub", "col", None)
    return jax.shard_map(
        on_device, mesh=mesh, in_specs=in_specs, out_specs=out_specs, check_vma=False
    )
```

profile of v0, /device:TPU:1, one launch (start us, length us, event | category | flops | bytes accessed | tf_op | source)
XLA Modules:
  0.0 1141.2 jit_solution(4845397803051537167)
XLA Ops:
  6.5 3.1 fusion.20
  10.5 151.3 %all-reduce.11.cloned.1.call-done = f32[1024,128]{1,0:T(8,128)} async-done(((f32[1024,128]{1,0:T(8,128)}), f32[1024,128]{1,0:T(8,128)}) %all-reduce.11.cloned.1.call-update) | async-done | bytes 524304 | tf_op jit(solution)/shard_map/psum | solution.py:89
  170.6 51.3 %all-reduce.13.cloned.1.call-done = f32[256,128]{0,1:T(8,128)} async-done(((f32[256,128]{0,1:T(8,128)}), f32[256,128]{0,1:T(8,128)}) %all-reduce.13.cloned.1.call-update) | async-done | bytes 131088 | tf_op jit(solution)/shard_map/psum | solution.py:64
  224.1 3.7 collective-permute-done.1
  227.8 4.7 fusion.12
  234.9 147.3 %all-reduce.15.cloned.1.call-done = f32[1024,128]{0,1:T(8,128)} async-done(((f32[1024,128]{0,1:T(8,128)}), f32[1024,128]{0,1:T(8,128)}) %all-reduce.15.cloned.1.call-update) | async-done | bytes 524304 | tf_op jit(solution)/shard_map/psum | solution.py:89
  388.5 4.2 collective-permute-done.2
  397.6 52.5 %all-reduce.17.cloned.1.call-done = f32[256,128]{0,1:T(8,128)} async-done(((f32[256,128]{0,1:T(8,128)}), f32[256,128]{0,1:T(8,128)}) %all-reduce.17.cloned.1.call-update) | async-done | bytes 131088 | tf_op jit(solution)/shard_map/psum | solution.py:64
  452.3 3.7 collective-permute-done.4
  459.0 5.7 collective-permute-done.5
  464.7 7.4 fusion.15
  472.1 150.5 %all-reduce.19.cloned.1.call-done = f32[1024,128]{0,1:T(8,128)} async-done(((f32[1024,128]{0,1:T(8,128)}), f32[1024,128]{0,1:T(8,128)}) %all-reduce.19.cloned.1.call-update) | async-done | bytes 524304 | tf_op jit(solution)/shard_map/psum | solution.py:89
  622.6 4.8 fusion
  630.2 4.0 collective-permute-done.6
  638.9 53.0 %all-reduce.21.cloned.1.call-done = f32[1,256,128]{1,2,0:T(8,128)} async-done(((f32[1,256,128]{1,2,0:T(8,128)}), f32[1,256,128]{1,2,0:T(8,128)}) %all-reduce.21.cloned.1.call-update) | async-done | bytes 131088 | tf_op jit(solution)/shard_map/psum | solution.py:64
  693.1 3.9 collective-permute-done.8
  700.9 5.6 collective-permute-done.9
  709.0 150.5 %all-reduce.23.cloned.1.call-done = f32[1024,128]{0,1:T(8,128)} async-done(((f32[1024,128]{0,1:T(8,128)}), f32[1024,128]{0,1:T(8,128)}) %all-reduce.23.cloned.1.call-update) | async-done | bytes 524304 | tf_op jit(solution)/shard_map/psum | solution.py:109
  859.4 3.2 fusion.6
  867.7 51.4 %all-reduce.25.cloned.1.call-done = f32[1,256,128]{1,2,0:T(8,128)} async-done(((f32[1,256,128]{1,2,0:T(8,128)}), f32[1,256,128]{1,2,0:T(8,128)}) %all-reduce.25.cloned.1.call-update) | async-done | bytes 131088 | tf_op jit(solution)/shard_map/psum | solution.py:64
  921.0 3.3 collective-permute-done.11
  929.0 149.6 %all-reduce.27.cloned.1.call-done = f32[1024,128]{1,0:T(8,128)} async-done(((f32[1024,128]{1,0:T(8,128)}), f32[1024,128]{1,0:T(8,128)}) %all-reduce.27.cloned.1.call-update) | async-done | bytes 524304 | tf_op jit(solution)/shard_map/psum | solution.py:109
  1078.6 3.1 convolution_bitcast_fusion.1
  1081.8 50.7 %all-reduce.29.cloned.1.call-done = f32[1,256,128]{1,2,0:T(8,128)} async-done(((f32[1,256,128]{1,2,0:T(8,128)}), f32[1,256,128]{1,2,0:T(8,128)}) %all-reduce.29.cloned.1.call-update) | async-done | bytes 131088 | tf_op jit(solution)/shard_map/psum | solution.py:64
  (91 shorter events, 58.8 us)
Async XLA Ops:
  6.5 163.9 %copy-start.2 = (f32[3,1,256,128]{3,2,1,0:T(8,128)S(1)}, f32[3,1,256,128]{3,2,1,0:T(8,128)}, u32[]{:S(2)}) copy-start(f32[3,1,256,128]{3,2,1,0:T(8,128)} %param.4) | copy-start | bytes 1179652
  6.5 155.3 %all-reduce.11.cloned.1.call-start = ((), (), s32[]{:S(2)}) async-start(), calls=%async_computation | async-start | bytes 1048576 | tf_op jit(solution)/shard_map/psum | solution.py:89
  9.6 223.0 %copy-start = (f32[3,1,128,1024]{3,2,1,0:T(8,128)S(1)}, f32[3,1,128,1024]{3,2,1,0:T(8,128)}, u32[]{:S(2)}) copy-start(f32[3,1,128,1024]{3,2,1,0:T(8,128)} %param.6) | copy-start | bytes 4718596
  9.6 212.3 %all-reduce.13.cloned.1.call-start = ((), (), s32[]{:S(2)}) async-start(), calls=%async_computation.1 | async-start | bytes 262144 | tf_op jit(solution)/shard_map/psum | solution.py:64
  165.4 4.3 collective-permute-start
  170.4 211.8 %all-reduce.15.cloned.1.call-start = ((), (), s32[]{:S(2)}) async-start(), calls=%async_computation.2 | async-start | bytes 1048576 | tf_op jit(solution)/shard_map/psum | solution.py:89
  222.8 5.0 collective-permute-start.1
  232.5 217.5 %all-reduce.17.cloned.1.call-start = ((), (), s32[]{:S(2)}) async-start(), calls=%async_computation.3 | async-start | bytes 262144 | tf_op jit(solution)/shard_map/psum | solution.py:64
  385.6 7.2 collective-permute-start.2
  392.8 3.9 collective-permute-start.3
  397.4 225.2 %all-reduce.19.cloned.1.call-start = ((), (), s32[]{:S(2)}) async-start(), calls=%async_computation.4 | async-start | bytes 1048576 | tf_op jit(solution)/shard_map/psum | solution.py:89
  451.0 5.0 collective-permute-start.4
  456.0 8.7 collective-permute-start.5
  472.1 219.8 %all-reduce.21.cloned.1.call-start = ((), (), s32[]{:S(2)}) async-start(), calls=%async_computation.5 | async-start | bytes 262144 | tf_op jit(solution)/shard_map/psum | solution.py:64
  627.4 6.8 collective-permute-start.6
  634.3 3.9 collective-permute-start.7
  638.9 220.5 %all-reduce.23.cloned.1.call-start = ((), (), s32[]{:S(2)}) async-start(), calls=%async_computation.6 | async-start | bytes 1048576 | tf_op jit(solution)/shard_map/psum | solution.py:109
  691.9 5.1 collective-permute-start.8
  698.1 8.5 collective-permute-start.9
  708.9 210.3 %all-reduce.25.cloned.1.call-start = ((), (), s32[]{:S(2)}) async-start(), calls=%async_computation.7 | async-start | bytes 262144 | tf_op jit(solution)/shard_map/psum | solution.py:64
  862.7 4.3 collective-permute-start.10
  867.7 210.9 %all-reduce.27.cloned.1.call-start = ((), (), s32[]{:S(2)}) async-start(), calls=%async_computation.8 | async-start | bytes 1048576 | tf_op jit(solution)/shard_map/psum | solution.py:109
  919.2 5.1 collective-permute-start.11
  928.9 203.6 %all-reduce.29.cloned.1.call-start = ((), (), s32[]{:S(2)}) async-start(), calls=%async_computation.9 | async-start | bytes 262144 | tf_op jit(solution)/shard_map/psum | solution.py:64
  (1 other events, 70.8 us)
Sparse Core Ops, SparseCore 0:
  9.9 151.8 all-reduce.10
  170.5 51.3 all-reduce.12
  232.7 149.4 all-reduce.14
  397.6 52.4 all-reduce.16
  472.2 150.3 all-reduce.18
  639.0 52.8 all-reduce.20
  709.0 150.3 all-reduce.22
  867.8 51.3 all-reduce.24
  929.0 149.5 all-reduce.26
  1081.8 50.5 all-reduce.28
where the time goes:
time: 1140 us
  waiting for transfers between devices  1050 us (92%)
  matrix products  35.2 us (3%)
  starting transfers between devices  22 us (2%)
  between operations  13.9 us (1%)
  other arithmetic  12.1 us (1%)
    psum x3, waiting for transfers between devices, on_device(): solved_panel = lax.psum(column_part, 'col')  449 us
    psum x2, waiting for transfers between devices, on_device(): residue = residue - lax.psum(correction, 'col')  300 us
    psum x5, waiting for transfers between devices, separator_sum(): own_part = lax.psum(own_part, 'row')  259 us
    ppermute x12, waiting for transfers between devices, swapped(): return lax.ppermute(value, axis, pairs)  45.3 us
  transfers between devices with their start and end apart: 22, of which 22 were waited for; matrix products, arithmetic and copies ran while one was open for 0% of the time, Pallas kernels for 0%

commit v1 on v0

--- a/solution.py
+++ b/solution.py
@@ -61,7 +61,7 @@
 
 def separator_sum(values, level_num, own_rhs):
     own_part = fold_halves(values, level_num)[0]
-    own_part = lax.psum(own_part, "row")
+    own_part = jnp.sum(lax.all_gather(own_part, "row"), axis=0)
     if own_rhs is not None:
         own_part = own_rhs - own_part
     return spread_panels(own_part[None], level_num)

time: 1140 us -> 962 us (0.84)
  waiting for transfers between devices: 1050 us -> 783 us
  blocking collectives: 0 us -> 97.7 us
    psum x5 -> x0, waiting for transfers between devices: 259 us -> none  [separator_sum(): own_part = lax.psum(own_part, 'row')]
    all_gather x0 -> x5, blocking collectives: none -> 97.7 us  [separator_sum(): own_part = jnp.sum(lax.all_gather(own_part, 'row'), axis=0)]
  transfers between devices with their start and end apart: 22 -> 17, of which waited for: 22 -> 17; matrix products, arithmetic and copies ran while one was open for 0% -> 0% of each run, Pallas kernels for 0% -> 0%
where the time goes in v1:
time: 962 us
  waiting for transfers between devices  783 us (81%)
  blocking collectives  97.7 us (10%)
  matrix products  34.6 us (4%)
  starting transfers between devices  22.2 us (2%)
  between operations  13.5 us (1%)
    psum x3, waiting for transfers between devices, on_device(): solved_panel = lax.psum(column_part, 'col')  443 us
    psum x2, waiting for transfers between devices, on_device(): residue = residue - lax.psum(correction, 'col')  295 us
    all_gather x5, blocking collectives, separator_sum(): own_part = jnp.sum(lax.all_gather(own_part, 'row'), axis=0)  97.7 us
    ppermute x12, waiting for transfers between devices, swapped(): return lax.ppermute(value, axis, pairs)  44.9 us
    ppermute x12, starting transfers between devices, swapped(): return lax.ppermute(value, axis, pairs)  22.1 us
  transfers between devices with their start and end apart: 17, of which 17 were waited for; matrix products, arithmetic and copies ran while one was open for 0% of the time, Pallas kernels for 0%

profile of v1, /device:TPU:1, one launch (start us, length us, event | category | flops | bytes accessed | tf_op | source)
XLA Modules:
  0.0 961.7 jit_solution(10729870303076769362)
XLA Ops:
  6.5 3.1 fusion.20
  10.5 151.3 %all-reduce.6.cloned.1.call-done = f32[1024,128]{1,0:T(8,128)} async-done(((f32[1024,128]{1,0:T(8,128)}), f32[1024,128]{1,0:T(8,128)}) %all-reduce.6.cloned.1.call-update) | async-done | bytes 524304 | tf_op jit(solution)/shard_map/psum | solution.py:89
  169.6 19.1 %all_gather.15 = f32[4,256,128]{2,1,0:T(8,128)S(1)} all-gather(f32[1,256,128]{2,1,0:T(8,128)S(1)} %bitcast_add_fusion.3), channel_id=1, replica_groups=mesh['sub'=4,'row'=4,'col'=16] {'row'}, dimensions={0}, use_global_device_ids=true | all-gather | bytes 655360 | tf_op jit(solution)/shard_map/all_gather | solution.py:64
  190.1 3.7 collective-permute-done.1
  193.8 4.7 fusion.12
  200.8 144.5 %all-reduce.8.cloned.1.call-done = f32[1024,128]{0,1:T(8,128)} async-done(((f32[1024,128]{0,1:T(8,128)}), f32[1024,128]{0,1:T(8,128)}) %all-reduce.8.cloned.1.call-update) | async-done | bytes 524304 | tf_op jit(solution)/shard_map/psum | solution.py:89
  351.4 4.4 collective-permute-done.2
  360.7 20.4 %all_gather.16 = f32[4,256,128]{2,1,0:T(8,128)S(1)} all-gather(f32[1,256,128]{2,1,0:T(8,128)S(1)} %dynamic-slice_add_fusion.1), channel_id=1, replica_groups=mesh['sub'=4,'row'=4,'col'=16] {'row'}, dimensions={0}, use_global_device_ids=true | all-gather | bytes 655360 | tf_op jit(solution)/shard_map/all_gather | solution.py:64
  382.5 3.7 collective-permute-done.4
  386.2 3.0 collective-permute-start.5
  389.2 5.6 collective-permute-done.5
  394.8 7.5 fusion.15
  402.3 147.7 %all-reduce.10.cloned.1.call-done = f32[1024,128]{0,1:T(8,128)} async-done(((f32[1024,128]{0,1:T(8,128)}), f32[1024,128]{0,1:T(8,128)}) %all-reduce.10.cloned.1.call-update) | async-done | bytes 524304 | tf_op jit(solution)/shard_map/psum | solution.py:89
  550.0 4.8 fusion
  558.5 4.1 collective-permute-done.6
  566.6 20.7 %all_gather.17 = f32[4,256,128]{2,1,0:T(8,128)S(1)} all-gather(f32[1,256,128]{2,1,0:T(8,128)S(1)} %dynamic-slice_add_fusion), channel_id=1, replica_groups=mesh['sub'=4,'row'=4,'col'=16] {'row'}, dimensions={0}, use_global_device_ids=true | all-gather | bytes 655360 | tf_op jit(solution)/shard_map/all_gather | solution.py:64
  588.6 3.7 collective-permute-done.8
  595.1 5.6 collective-permute-done.9
  602.9 147.7 %all-reduce.12.cloned.1.call-done = f32[1024,128]{0,1:T(8,128)} async-done(((f32[1024,128]{0,1:T(8,128)}), f32[1024,128]{0,1:T(8,128)}) %all-reduce.12.cloned.1.call-update) | async-done | bytes 524304 | tf_op jit(solution)/shard_map/psum | solution.py:109
  750.7 3.1 fusion.6
  758.2 19.1 %all_gather.18 = f32[4,256,128]{2,1,0:T(8,128)S(1)} all-gather(f32[1,256,128]{2,1,0:T(8,128)S(1)} %copy.31), channel_id=1, replica_groups=mesh['sub'=4,'row'=4,'col'=16] {'row'}, dimensions={0}, use_global_device_ids=true | all-gather | bytes 655360 | tf_op jit(solution)/shard_map/all_gather | solution.py:64
  779.5 3.0 collective-permute-done.11
  786.1 146.9 %all-reduce.14.cloned.1.call-done = f32[1024,128]{1,0:T(8,128)} async-done(((f32[1024,128]{1,0:T(8,128)}), f32[1024,128]{1,0:T(8,128)}) %all-reduce.14.cloned.1.call-update) | async-done | bytes 524304 | tf_op jit(solution)/shard_map/psum | solution.py:109
  935.4 18.4 %all-gather = f32[1024,128]{0,1:T(8,128)S(1)} all-gather(f32[256,128]{0,1:T(8,128)S(1)} %convolution_bitcast_fusion.1), channel_id=2, replica_groups=mesh['sub'=4,'row'=4,'col'=16] {'row'}, dimensions={0}, use_global_device_ids=true | all-gather | bytes 655360 | tf_op jit(solution)/shard_map/all_gather | solution.py:64
  (83 shorter events, 52.7 us)
Async XLA Ops:
  6.5 182.2 %copy-start.3 = (f32[3,1,256,128]{3,2,1,0:T(8,128)S(1)}, f32[3,1,256,128]{3,2,1,0:T(8,128)}, u32[]{:S(2)}) copy-start(f32[3,1,256,128]{3,2,1,0:T(8,128)} %param.4) | copy-start | bytes 1179652
  6.5 155.3 %all-reduce.6.cloned.1.call-start = ((), (), s32[]{:S(2)}) async-start(), calls=%async_computation | async-start | bytes 1048576 | tf_op jit(solution)/shard_map/psum | solution.py:89
  9.6 189.0 %copy-start = (f32[3,1,128,1024]{3,2,1,0:T(8,128)S(1)}, f32[3,1,128,1024]{3,2,1,0:T(8,128)}, u32[]{:S(2)}) copy-start(f32[3,1,128,1024]{3,2,1,0:T(8,128)} %param.6) | copy-start | bytes 4718596
  9.6 335.7 %all-reduce.8.cloned.1.call-start = ((), (), s32[]{:S(2)}) async-start(), calls=%async_computation.1 | async-start | bytes 1048576 | tf_op jit(solution)/shard_map/psum | solution.py:89
  161.8 36.8 %copy-start.1 = (f32[1024,128]{1,0:T(8,128)S(1)}, f32[1024,128]{1,0:T(8,128)}, u32[]{:S(2)}) copy-start(f32[1024,128]{1,0:T(8,128)} %all-reduce.6.cloned.1.call-done) | copy-start | bytes 1572868
  165.3 4.3 collective-permute-start
  188.8 5.0 collective-permute-start.1
  198.5 351.5 %all-reduce.10.cloned.1.call-start = ((), (), s32[]{:S(2)}) async-start(), calls=%async_computation.2 | async-start | bytes 1048576 | tf_op jit(solution)/shard_map/psum | solution.py:89
  348.6 7.2 collective-permute-start.2
  356.8 3.9 collective-permute-start.3
  381.2 5.0 collective-permute-start.4
  386.2 8.6 collective-permute-start.5
  402.3 348.4 %all-reduce.12.cloned.1.call-start = ((), (), s32[]{:S(2)}) async-start(), calls=%async_computation.3 | async-start | bytes 1048576 | tf_op jit(solution)/shard_map/psum | solution.py:109
  554.8 195.9 %copy-start.2 = (f32[1024,128]{0,1:T(8,128)S(1)}, f32[1024,128]{0,1:T(8,128)}, u32[]{:S(2)}) copy-start(f32[1024,128]{0,1:T(8,128)} %all-reduce.8.cloned.1.call-done) | copy-start | bytes 1572868
  555.7 6.9 collective-permute-start.6
  562.7 3.9 collective-permute-start.7
  587.3 5.0 collective-permute-start.8
  592.3 8.4 collective-permute-start.9
  602.9 330.1 %all-reduce.14.cloned.1.call-start = ((), (), s32[]{:S(2)}) async-start(), calls=%async_computation.4 | async-start | bytes 1048576 | tf_op jit(solution)/shard_map/psum | solution.py:109
  753.8 4.3 collective-permute-start.10
  777.3 5.2 collective-permute-start.11
Sparse Core Ops, SparseCore 0:
  9.9 151.8 all-reduce.5
  198.6 146.6 all-reduce.7
  402.4 147.5 all-reduce.9
  603.0 147.5 all-reduce.11
  786.2 146.7 all-reduce.13
